TPU v7x, 32 devices: a whole 2x2x4 slice. The times are simulated.
32 devices in a mesh: depth: 8 (over y, x, core), group: 4 (over z).
Axes of the slice: x: 2, y: 2, z: 4, core: 2. Of those that a mesh axis runs over, the one named last changes fastest.
Arguments:
- output_one: bfloat16 [32, 128, 64, 128], P(None, 'depth', 'group'), may hold values from -6 to 6
- output_two: bfloat16 [32, 128, 64, 128], P(None, 'depth', 'group'), may hold values from -6 to 6
- cotangent_one: bfloat16 [32, 128, 64, 128], P(None, 'depth', 'group'), may hold values from -6 to 6
- cotangent_two: bfloat16 [32, 128, 64, 128], P(None, 'depth', 'group'), may hold values from -6 to 6
- first_weight: bfloat16 [27, 32, 32], replicated, may hold values from -0.21875 to 0.21875
- second_weight: bfloat16 [27, 32, 32], replicated, may hold values from -0.21875 to 0.21875
- bricks: int32 [8, 4, 8], P('depth'), may hold values from 0 to 8, as said below
Outputs:
- restored_one: bfloat16 [32, 128, 64, 128], P(None, 'depth', 'group')
- restored_two: bfloat16 [32, 128, 64, 128], P(None, 'depth', 'group')
- input_grad_one: bfloat16 [32, 128, 64, 128], P(None, 'depth', 'group')
- input_grad_two: bfloat16 [32, 128, 64, 128], P(None, 'depth', 'group')
- first_weight_grad: float32 [27, 32, 32], replicated
- second_weight_grad: float32 [27, 32, 32], replicated
Inputs may be any that keep to these rules, and one draw needn't show every extreme that they name: bricks[z, g, :] lists the positions of the occupied bricks of depth layer z and lateral row g, distinct and ascending, followed by 8 in every unused entry. For each z the numbers of occupied bricks over g = 0 .. 3 are a reordering of 1 + (7 * j * j) // 9 for j = 0 .. 3, so in every depth layer one row has all 8 bricks occupied and the layer holds at most 16 occupied bricks.
All inputs are finite; a program needn't handle non-finite values.
Results may differ from a plain program's by a relative error of at most 0.0085.
Values may be sent and summed in bfloat16 or wider, within the bound.
No kernel may reach another device: no remote copies, remote signals or barrier semaphores. Data moves between devices by JAX's collectives and lax.ppermute only.
A program may use at most 256 MiB of HBM per device.

v0:
```python
import math
import jax
import jax.numpy as jnp
from jax import lax
from jax.sharding import PartitionSpec as P


def extended_2(shard, sides, width):
    for axis, dim in sides:
        size, length = (lax.axis_size(axis), shard.shape[dim])
        up = [(i, (i + 1) % size) for i in range(size - 1)]
        down = [(j, i) for i, j in up]
        last = lax.slice_in_dim(shard, length - width, length, axis=dim)
        initial = lax.slice_in_dim(shard, 0, width, axis=dim)
        before = lax.ppermute(last, axis, up)
        after = lax.ppermute(initial, axis, down)
        shard = jnp.concatenate([before, shard, after], axis=dim)
    return shard


def logistic_slope(inputs):
    logistic = jax.nn.sigmoid(inputs)
    return logistic * (1.0 + inputs * (1.0 - logistic))


def tap_offsets(brick_edge):
    window_edge = brick_edge + 2
    offsets = []
    for depth_step in range(3):
        for row_step in range(3):
            for col_step in range(3):
                offsets.append(
                    depth_step * window_edge * window_edge + row_step * window_edge + col_step
                )
    return offsets


def grid_length(brick_edge):
    window_edge = brick_edge + 2
    return (
        (brick_edge - 1) * window_edge * window_edge + (brick_edge - 1) * window_edge + brick_edge
    )


def padded_length(brick_edge):
    return (grid_length(brick_edge) + 127) // 128 * 128


def extend(window, brick_edge):
    needed = max(tap_offsets(brick_edge)) + padded_length(brick_edge)
    return jnp.pad(window, ((0, 0), (0, max(needed - window.shape[1], 0))))


def convolve(window, kernel, brick_edge):
    length = padded_length(brick_edge)
    total = jnp.zeros((kernel.shape[1], length), jnp.float32)
    for number, offset in enumerate(tap_offsets(brick_edge)):
        total = total + jnp.dot(
            kernel[number], window[:, offset : offset + length], preferred_element_type=jnp.float32
        )
    return total


def grid_to_brick(values, brick_edge):
    window_edge = brick_edge + 2
    channels = values.shape[0]
    full_size = brick_edge * window_edge * window_edge
    values = values[:, : grid_length(brick_edge)]
    padded = jnp.pad(values, ((0, 0), (0, full_size - values.shape[1])))
    cubes = padded.reshape(channels, brick_edge, window_edge, window_edge)[
        :, :, :brick_edge, :brick_edge
    ]
    return cubes.reshape(channels, brick_edge**3)


def brick_to_grid(values, brick_edge):
    channels = values.shape[0]
    cubes = values.reshape(channels, brick_edge, brick_edge, brick_edge)
    padded = jnp.pad(cubes, ((0, 0), (0, 0), (0, 2), (0, 2)))
    grid = padded.reshape(channels, -1)[:, : grid_length(brick_edge)]
    return jnp.pad(grid, ((0, 0), (0, padded_length(brick_edge) - grid_length(brick_edge))))


def centre(window, brick_edge):
    window_edge = brick_edge + 2
    offset = window_edge * window_edge + window_edge + 1
    return grid_to_brick(window[:, offset : offset + grid_length(brick_edge)], brick_edge)


def weight_gradient(errors, window, brick_edge):
    grid = brick_to_grid(errors, brick_edge)
    length = padded_length(brick_edge)
    pieces = []
    for offset in tap_offsets(brick_edge):
        pieces.append(
            lax.dot_general(
                grid,
                window[:, offset : offset + length],
                (((1,), (1,)), ((), ())),
                preferred_element_type=jnp.float32,
            )
        )
    return jnp.stack(pieces, axis=0)


def first_round(windows, kernels, brick_edge):
    source = extend(windows[0], brick_edge)
    preact = grid_to_brick(convolve(source, kernels[1], brick_edge), brick_edge)
    cotangent = centre(windows[1], brick_edge).astype(jnp.float32)
    shaped = jax.nn.silu(preact).astype(jnp.bfloat16)
    errors = (cotangent * logistic_slope(preact)).astype(jnp.bfloat16)
    return (jnp.stack([shaped, errors]), weight_gradient(errors, source, brick_edge))


def second_round(windows, kernels, brick_edge):
    source = extend(windows[0], brick_edge)
    preact = grid_to_brick(convolve(source, kernels[0], brick_edge), brick_edge)
    spread = grid_to_brick(
        convolve(extend(windows[1], brick_edge), kernels[3], brick_edge), brick_edge
    )
    totals = (centre(windows[2], brick_edge).astype(jnp.float32) + spread).astype(jnp.bfloat16)
    shaped = jax.nn.silu(preact).astype(jnp.bfloat16)
    errors = (totals.astype(jnp.float32) * logistic_slope(preact)).astype(jnp.bfloat16)
    return (jnp.stack([totals, shaped, errors]), weight_gradient(errors, source, brick_edge))


def third_round(windows, kernels, brick_edge):
    spread = grid_to_brick(
        convolve(extend(windows[0], brick_edge), kernels[2], brick_edge), brick_edge
    )
    result = (centre(windows[1], brick_edge).astype(jnp.float32) + spread).astype(jnp.bfloat16)
    channels = result.shape[0]
    return (result[None], jnp.zeros((27, channels, channels), jnp.float32))


def cut_window(padded, offset, brick_edge):
    window_edge = brick_edge + 2
    anchor = jnp.zeros((), jnp.int32)
    block = lax.dynamic_slice(
        padded,
        (anchor, anchor, anchor, anchor, offset),
        (padded.shape[0], padded.shape[1], window_edge, window_edge, window_edge),
    )
    return block.reshape(padded.shape[0], padded.shape[1], window_edge**3)


def with_faces(stacked):
    extended = extended_2(stacked, (("depth", 2), ("group", 3)), 1)
    return jnp.pad(extended, ((0, 0), (0, 0), (0, 0), (0, 0), (1, 1)))


def zero_rim(volume):
    return jnp.pad(volume[None], ((0, 0), (0, 0), (1, 1), (1, 1), (1, 1)))


def own_pass(padded, initial, compute, own_list, own_count, brick_edge, grad_shape):

    def visit(number, state):
        slab_stack, partials = state
        offset = own_list[number] * brick_edge
        bricks_out, gradient = compute(cut_window(padded, offset, brick_edge))
        cubes = bricks_out.reshape(
            bricks_out.shape[0], bricks_out.shape[1], brick_edge, brick_edge, brick_edge
        )
        anchor = jnp.zeros((), jnp.int32)
        slab_stack = lax.dynamic_update_slice(
            slab_stack, cubes, (anchor, anchor, anchor, anchor, offset)
        )
        return (slab_stack, partials + gradient)

    return lax.fori_loop(0, own_count, visit, (initial, jnp.zeros(grad_shape, jnp.float32)))


def local(
    output_one, output_two, cotangent_one, cotangent_two, first_weight, second_weight, bricks
):
    brick_edge = output_one.shape[1]
    across = output_one.shape[3]
    slots = bricks.shape[2]
    groups = lax.axis_size("group")
    position = lax.axis_index("group")
    listing = bricks[0]
    counts = jnp.sum((listing < slots).astype(jnp.int32), axis=1)
    own_list = listing[position]
    own_count = counts[position]
    present = jnp.any(own_list[:, None] == jnp.arange(slots, dtype=jnp.int32)[None, :], axis=0)
    column_mask = jnp.repeat(present.astype(jnp.float32), brick_edge)
    kernels = (
        first_weight,
        second_weight,
        jnp.transpose(jnp.flip(first_weight, 0), (0, 2, 1)),
        jnp.transpose(jnp.flip(second_weight, 0), (0, 2, 1)),
    )
    grad_shape = first_weight.shape

    def run_round(padded, initial, compute):
        return own_pass(padded, initial, compute, own_list, own_count, brick_edge, grad_shape)

    zeros_volume = jnp.zeros_like(output_one)
    upper_masked = (output_one.astype(jnp.float32) * column_mask).astype(jnp.bfloat16)
    padded = jnp.concatenate([with_faces(upper_masked[None]), zero_rim(cotangent_two)], axis=0)
    first_stack, second_partial = run_round(
        padded,
        jnp.stack([zeros_volume, zeros_volume]),
        lambda windows: first_round(windows, kernels, brick_edge),
    )
    restored_two = (output_two.astype(jnp.float32) - first_stack[0].astype(jnp.float32)).astype(
        jnp.bfloat16
    )
    lower_masked = (restored_two.astype(jnp.float32) * column_mask).astype(jnp.bfloat16)
    padded = jnp.concatenate(
        [with_faces(jnp.stack([lower_masked, first_stack[1]])), zero_rim(cotangent_one)], axis=0
    )
    second_stack, first_partial = run_round(
        padded,
        jnp.stack([cotangent_one, zeros_volume, zeros_volume]),
        lambda windows: second_round(windows, kernels, brick_edge),
    )
    input_grad_one = second_stack[0]
    restored_one = (output_one.astype(jnp.float32) - second_stack[1].astype(jnp.float32)).astype(
        jnp.bfloat16
    )
    padded = jnp.concatenate([with_faces(second_stack[2][None]), zero_rim(cotangent_two)], axis=0)
    third_stack, unused = run_round(
        padded, cotangent_two[None], lambda windows: third_round(windows, kernels, brick_edge)
    )
    input_grad_two = third_stack[0]
    first_total, second_total = lax.psum((first_partial, second_partial), ("depth", "group"))
    scale = 1.0 / math.sqrt(
        float(brick_edge * lax.axis_size("depth") * brick_edge * groups * across)
    )
    return (
        restored_one,
        restored_two,
        input_grad_one,
        input_grad_two,
        first_total * scale,
        second_total * scale,
    )


def solution(mesh):
    placed = (
        P(None, "depth", "group", None),
        P(None, "depth", "group", None),
        P(None, "depth", "group", None),
        P(None, "depth", "group", None),
        P(),
        P(),
        P("depth", None, None),
    )
    return jax.shard_map(
        local,
        mesh=mesh,
        in_specs=placed,
        out_specs=(
            P(None, "depth", "group", None),
            P(None, "depth", "group", None),
            P(None, "depth", "group", None),
            P(None, "depth", "group", None),
            P(),
            P(),
        ),
        check_vma=False,
    )
```

profile of v0, /device:TPU:0, one launch (start us, length us, event | category | flops | bytes accessed | tf_op | source)
XLA Modules:
  0.0 2359.1 jit_solution(11144788152635191099)
XLA Ops:
  29.5 6.9 select_maximum_fusion.6
  36.4 9.6 fusion.928
  46.1 22.5 copy.67
  68.5 6.4 broadcast.173
  75.7 612.9 %while.40 = (s32[]{:T(128)}, bf16[2,32,16,16,128]{1,4,3,2,0:T(8,128)(2,1)}, f32[27,32,32]{2,1,0:T(8,128)}, s32[]{:T(128)}, s32[8]{0:T(128)S(1)}, /*index=5*/bf16...) while((s32[]{:T(128)}, ...), condition=%wide.region_3.4_spmd, body=%wide.region_2.3_spmd.sunk | while | flops 587555840 | bytes 164357712 | solution.py:171
  100.9 6.3 constant_dynamic-slice_fusion.10
  173.7 6.3 constant_dynamic-slice_fusion.10
  246.5 6.3 constant_dynamic-slice_fusion.10
  319.2 6.3 constant_dynamic-slice_fusion.10
  688.6 15.1 copy.68
  715.4 7.9 collective-permute-start.6
  739.5 17.1 stack.360.clone
  763.0 14.0 select_maximum_fusion
  777.0 6.8 fusion.920
  783.9 33.0 %copy.72 = bf16[3,32,18,18,130]{1,4,3,2,0:T(8,128)(2,1)} copy(bf16[3,32,18,18,130]{4,1,3,2,0:T(8,128)(2,1)} %fusion.920) | data formatting | bytes 16174080 | tf_op jit(solution)/shard_map/while | solution.py:171
  817.7 965.3 %while.41 = (s32[]{:T(128)}, bf16[3,32,16,16,128]{1,4,3,2,0:T(8,128)(2,1)}, f32[27,32,32]{2,1,0:T(8,128)}, s32[]{:T(128)}, s32[8]{0:T(128)S(1)}, /*index=5*/bf16...) while((s32[]{:T(128)}, ...), condition=%wide.region_5.6_spmd, body=%wide.region_4.5_spmd.sunk | while | flops 883973120 | bytes 240212160 | solution.py:171
  819.9 8.9 constant_dynamic-slice_fusion.11
  939.7 8.9 constant_dynamic-slice_fusion.11
  1059.3 9.0 constant_dynamic-slice_fusion.11
  1179.0 9.0 constant_dynamic-slice_fusion.11
  1298.6 8.9 constant_dynamic-slice_fusion.11
  1418.1 8.9 constant_dynamic-slice_fusion.11
  1537.8 8.9 constant_dynamic-slice_fusion.11
  1657.4 8.3 constant_dynamic-slice_fusion.11
  1783.1 22.0 copy.73
  1810.4 23.4 copy.74
  1849.0 134.6 %all-reduce.20.cloned.1.call-done = (f32[27,32,32]{2,1,0:T(8,128)}, f32[27,32,32]{2,1,0:T(8,128)}) async-done(((f32[27,32,32]{2,1,0:T(8,128)}, f32[27,32,32]{2,1,0:T(8,128)}), (f32[27,32,32]{2,1,0:T(8,128)}, f32[27,32,32]{2,1,0:T(8,128)})) %all-reduce.20.cloned.1.call-update) | async-done | bytes 221200 | tf_op jit(solution)/shard_map/psum | solution.py:228
  1985.8 8.2 select_maximum_fusion.2
  1994.0 9.6 fusion.929
  2003.6 22.5 copy.80
  2026.1 317.2 %while.42 = (s32[]{:T(128)}, bf16[1,32,16,16,128]{1,4,3,2,0:T(8,128)(2,1)}, s32[]{:T(128)}, s32[8]{0:T(128)S(1)}, bf16[2,32,18,18,130]{1,4,3,2,0:T(8,128)(2,1)},...) while((s32[]{:T(128)}, ...), condition=%wide.region_7.8_spmd, body=%wide.region_6.7_spmd.sunk | while | flops 295106560 | bytes 87847184 | solution.py:171
  2343.3 8.6 copy.81
  (1937 shorter events, 1796.6 us)
Async XLA Ops:
  7.2 1976.5 %all-reduce.20.cloned.1.call-start = ((), (), s32[]{:S(2)}) async-start(), calls=%async_computation | async-start | bytes 1769472 | tf_op jit(solution)/shard_map/psum | solution.py:228
  11.1 7.8 copy-start.16
  11.2 3.7 collective-permute-start
  13.6 5.3 collective-permute-start.1
  19.0 8.8 collective-permute-start.2
  22.5 7.0 collective-permute-start.3
  23.8 5.7 copy-start.17
  26.9 9.6 copy-start.5
  688.6 17.2 copy-start.26
  688.6 17.2 copy-start.28
  706.5 8.0 copy-start.8
  709.6 4.9 copy-start.10
  709.7 2.8 collective-permute-start.4
  711.0 13.6 copy-start.23
  711.0 3.6 collective-permute-start.5
  714.6 10.2 copy-start.6
  715.4 47.6 %collective-permute-start.6 = (bf16[2,32,18,1,128]{4,1,3,2,0:T(8,128)(2,1)}, bf16[2,32,18,1,128]{4,1,3,2,0:T(8,128)(2,1)}, u32[]{:S(2)}, u32[]{:S(2)}) collective-permute-start(bf16[2,32,18,1,128]{4,1,3,2,0:T(8,128)(2,1)} %get-tuple-element.429), channel_id=1, source_target_pairs={{0,1},{1,2},{2,3},{4,5},{5,6},{6,7},{8,9},{9,10},{10,11},{12,13},{... | collective-permute-start | bytes 884744 | tf_op jit(solution)/shard_map/ppermute | solution.py:15
  723.3 39.7 %collective-permute-start.7 = (bf16[2,32,18,1,128]{4,1,3,2,0:T(8,128)(2,1)S(1)}, bf16[2,32,18,1,128]{4,1,3,2,0:T(8,128)(2,1)}, u32[]{:S(2)}, u32[]{:S(2)}) collective-permute-start(bf16[2,32,18,1,128]{4,1,3,2,0:T(8,128)(2,1)S(1)} %get-tuple-element.430), channel_id=1, source_target_pairs={{1,0},{2,1},{3,2},{5,4},{6,5},{7,6},{9,8},{10,9},{11,10},{13,12},{... | collective-permute-start | bytes 884744 | tf_op jit(solution)/shard_map/ppermute | solution.py:16
  1783.0 23.0 copy-start.20
  1833.8 10.5 collective-permute-start.8
  1835.1 9.2 collective-permute-start.9
  1844.4 141.4 %collective-permute-start.10 = (bf16[1,32,18,1,128]{4,1,3,2,0:T(8,128)(2,1)S(1)}, bf16[1,32,18,1,128]{4,1,3,2,0:T(8,128)(2,1)S(1)}, u32[]{:S(2)}, u32[]{:S(2)}) collective-permute-start(bf16[1,32,18,1,128]{4,1,3,2,0:T(8,128)(2,1)S(1)} %get-tuple-element.433), channel_id=1, source_target_pairs={{0,1},{1,2},{2,3},{4,5},{5,6},{6,7},{8,9},{9,10},{10,11},{12,13},{... | collective-permute-start | bytes 442376 | tf_op jit(solution)/shard_map/ppermute | solution.py:15
  1847.7 138.1 %collective-permute-start.11 = (bf16[1,32,18,1,128]{4,1,3,2,0:T(8,128)(2,1)S(1)}, bf16[1,32,18,1,128]{4,1,3,2,0:T(8,128)(2,1)S(1)}, u32[]{:S(2)}, u32[]{:S(2)}) collective-permute-start(bf16[1,32,18,1,128]{4,1,3,2,0:T(8,128)(2,1)S(1)} %get-tuple-element.434), channel_id=1, source_target_pairs={{1,0},{2,1},{3,2},{5,4},{6,5},{7,6},{9,8},{10,9},{11,10},{13,12},{... | collective-permute-start | bytes 442376 | tf_op jit(solution)/shard_map/ppermute | solution.py:16
  1985.8 8.2 copy-start.7
  2058.2 5.1 copy-start
  2097.8 5.1 copy-start
  2137.4 5.1 copy-start
  2176.9 5.1 copy-start
  2216.5 5.1 copy-start
  2256.0 5.1 copy-start
  2295.6 5.1 copy-start
  2334.7 5.1 copy-start
  (95 other events, 208.8 us)
Sparse Core Ops, SparseCore 0:
  1844.4 139.1 all-reduce.19
where the time goes:
time: 2390 us; the launch traced here: 2360 us
  matrix products  934 us (39%)
  local copies, waits for them, and re-layouts  918 us (38%)
  other arithmetic  239 us (10%)
  waiting for transfers between devices  142 us (6%)
  loops' own time  83.2 us (3%)
  starting transfers between devices  27.6 us (1%)
    dot_general x864, matrix products, convolve(): jnp.dot(kernel[number], window[:, offset:offset + length], preferred_elem...  639 us
    dot_general x432, matrix products, weight_gradient(): lax.dot_general(grid, window[:, offset:offset + length], (((1,), (1,)), (...  296 us
    reshape x56, local copies, waits for them, and re-layouts, grid_to_brick(): padded.reshape(channels, brick_edge, window_edge, window_edge)  169 us
    while x8, local copies, waits for them, and re-layouts, own_pass(): lax.fori_loop(0, own_count, visit, (initial, jnp.zeros(grad_shape, jnp.fl...  153 us
    psum x1, waiting for transfers between devices, local(): lax.psum((first_partial, second_partial), ('depth', 'group'))  135 us
    pad x56, local copies, waits for them, and re-layouts, grid_to_brick(): padded = jnp.pad(values, ((0, 0), (0, full_size - values.shape[1])))  84.9 us
    another operation x3, loops' own time, own_pass(): lax.fori_loop(0, own_count, visit, (initial, jnp.zeros(grad_shape, jnp.fl...  83.2 us
    slice x8, local copies, waits for them, and re-layouts, second_round(): windows[2]  71 us
  transfers between devices with their start and end apart: 13, of which 4 were waited for; matrix products, arithmetic and copies ran while one was open for 2% of the time, Pallas kernels for 0%

commit v1 on v0

--- a/solution.py
+++ b/solution.py
@@ -225,7 +225,9 @@
         padded, cotangent_two[None], lambda windows: third_round(windows, kernels, brick_edge)
     )
     input_grad_two = third_stack[0]
-    first_total, second_total = lax.psum((first_partial, second_partial), ("depth", "group"))
+    first_total, second_total = lax.psum(
+        lax.psum((first_partial, second_partial), "group"), "depth"
+    )
     scale = 1.0 / math.sqrt(
         float(brick_edge * lax.axis_size("depth") * brick_edge * groups * across)
     )

time: 2390 us -> 2300 us (0.962)
  waiting for transfers between devices: 142 us -> 56.4 us
    psum x1 -> x2, waiting for transfers between devices: 135 us -> 48.5 us  [the longest x1 48.5 us: local(): lax.psum((first_partial, second_partial), 'group')]
  transfers between devices with their start and end apart: 13 -> 14, of which waited for: 4 -> 4; matrix products, arithmetic and copies ran while one was open for 2% -> 19% of each run, Pallas kernels for 0% -> 0%
where the time goes in v1:
time: 2300 us; the launch traced here: 2270 us
  matrix products  934 us (41%)
  local copies, waits for them, and re-layouts  919 us (40%)
  other arithmetic  239 us (10%)
  loops' own time  81.6 us (4%)
  waiting for transfers between devices  56.4 us (2%)
  starting transfers between devices  25.8 us (1%)
    dot_general x864, matrix products, convolve(): jnp.dot(kernel[number], window[:, offset:offset + length], preferred_elem...  639 us
    dot_general x432, matrix products, weight_gradient(): lax.dot_general(grid, window[:, offset:offset + length], (((1,), (1,)), (...  296 us
    reshape x56, local copies, waits for them, and re-layouts, grid_to_brick(): padded.reshape(channels, brick_edge, window_edge, window_edge)  169 us
    while x8, local copies, waits for them, and re-layouts, own_pass(): lax.fori_loop(0, own_count, visit, (initial, jnp.zeros(grad_shape, jnp.fl...  154 us
    pad x56, local copies, waits for them, and re-layouts, grid_to_brick(): padded = jnp.pad(values, ((0, 0), (0, full_size - values.shape[1])))  84.8 us
    another operation x3, loops' own time, own_pass(): lax.fori_loop(0, own_count, visit, (initial, jnp.zeros(grad_shape, jnp.fl...  81.6 us
    slice x8, local copies, waits for them, and re-layouts, second_round(): windows[2]  71.1 us
    dynamic_update_slice x24, other arithmetic, visit(): lax.dynamic_update_slice(slab_stack, cubes, (anchor, anchor, anchor, anch...  66.9 us
  transfers between devices with their start and end apart: 14, of which 4 were waited for; matrix products, arithmetic and copies ran while one was open for 19% of the time, Pallas kernels for 0%

profile of v1, /device:TPU:0, one launch (start us, length us, event | category | flops | bytes accessed | tf_op | source)
XLA Modules:
  0.0 2270.8 jit_solution(11013892018252633689)
XLA Ops:
  29.5 6.9 select_maximum_fusion.6
  36.4 9.6 fusion.928
  46.0 22.5 copy.67
  68.5 6.4 broadcast.173
  75.7 612.5 %while.40 = (s32[]{:T(128)}, bf16[2,32,16,16,128]{1,4,3,2,0:T(8,128)(2,1)}, f32[27,32,32]{2,1,0:T(8,128)}, s32[]{:T(128)}, s32[8]{0:T(128)S(1)}, /*index=5*/bf16...) while((s32[]{:T(128)}, ...), condition=%wide.region_3.4_spmd, body=%wide.region_2.3_spmd.sunk | while | flops 587555840 | bytes 164357712 | solution.py:171
  173.6 6.4 constant_dynamic-slice_fusion.10
  391.7 6.4 constant_dynamic-slice_fusion.10
  688.2 15.1 copy.68
  715.0 7.9 collective-permute-start.6
  739.1 17.1 stack.360.clone
  762.6 14.0 select_maximum_fusion
  776.6 6.9 fusion.920
  783.5 33.0 %copy.72 = bf16[3,32,18,18,130]{1,4,3,2,0:T(8,128)(2,1)} copy(bf16[3,32,18,18,130]{4,1,3,2,0:T(8,128)(2,1)} %fusion.920) | data formatting | bytes 16174080 | tf_op jit(solution)/shard_map/while | solution.py:171
  817.3 964.9 %while.41 = (s32[]{:T(128)}, bf16[3,32,16,16,128]{1,4,3,2,0:T(8,128)(2,1)}, f32[27,32,32]{2,1,0:T(8,128)}, s32[]{:T(128)}, s32[8]{0:T(128)S(1)}, /*index=5*/bf16...) while((s32[]{:T(128)}, ...), condition=%wide.region_5.6_spmd, body=%wide.region_4.5_spmd.sunk | while | flops 883973120 | bytes 240212160 | solution.py:171
  819.4 9.0 constant_dynamic-slice_fusion.11
  939.2 9.0 constant_dynamic-slice_fusion.11
  1058.7 9.0 constant_dynamic-slice_fusion.11
  1178.3 9.0 constant_dynamic-slice_fusion.11
  1297.9 8.9 constant_dynamic-slice_fusion.11
  1417.4 8.9 constant_dynamic-slice_fusion.11
  1537.0 8.9 constant_dynamic-slice_fusion.11
  1656.6 8.3 constant_dynamic-slice_fusion.11
  1782.2 22.0 copy.73
  1814.2 24.2 %copy.74 = bf16[3,32,16,16,128]{4,3,2,1,0:T(8,128)(2,1)} copy(bf16[3,32,16,16,128]{1,4,3,2,0:T(8,128)(2,1)} %get-tuple-element.288) | data formatting | bytes 12582912 | tf_op jit(solution)/shard_map/while | solution.py:171
  1846.9 48.5 %all-reduce.24.cloned.1.call-done = (f32[27,32,32]{2,1,0:T(8,128)}, f32[27,32,32]{2,1,0:T(8,128)}) async-done(((f32[27,32,32]{2,1,0:T(8,128)}, f32[27,32,32]{2,1,0:T(8,128)}), (f32[27,32,32]{2,1,0:T(8,128)}, f32[27,32,32]{2,1,0:T(8,128)})) %all-reduce.24.cloned.1.call-update) | async-done | bytes 221200 | tf_op jit(solution)/shard_map/psum | solution.py:229
  1895.5 8.2 select_maximum_fusion.2
  1903.6 9.6 fusion.929
  1913.2 22.5 copy.80
  1935.8 317.0 %while.42 = (s32[]{:T(128)}, bf16[1,32,16,16,128]{1,4,3,2,0:T(8,128)(2,1)}, s32[]{:T(128)}, s32[8]{0:T(128)S(1)}, bf16[2,32,18,18,130]{1,4,3,2,0:T(8,128)(2,1)},...) while((s32[]{:T(128)}, ...), condition=%wide.region_7.8_spmd, body=%wide.region_6.7_spmd.sunk | while | flops 295106560 | bytes 87847184 | solution.py:171
  1977.4 6.4 constant_dynamic-slice_fusion.12
  2096.0 6.4 constant_dynamic-slice_fusion.12
  2252.8 8.6 copy.81
  (1940 shorter events, 1794.7 us)
Async XLA Ops:
  7.2 1888.2 %all-reduce.24.cloned.1.call-start = ((), (), s32[]{:S(2)}) async-start(), calls=%async_computation.1 | async-start | bytes 1769472 | tf_op jit(solution)/shard_map/psum | solution.py:229
  11.1 7.8 copy-start.16
  11.2 3.7 collective-permute-start
  13.6 5.3 collective-permute-start.1
  19.0 8.8 collective-permute-start.2
  22.5 7.0 collective-permute-start.3
  23.8 5.7 copy-start.17
  26.9 9.5 copy-start.5
  688.2 17.2 copy-start.26
  688.2 17.2 copy-start.28
  706.1 8.0 copy-start.8
  709.3 2.8 collective-permute-start.4
  710.6 13.6 copy-start.23
  710.6 3.6 collective-permute-start.5
  714.2 10.2 copy-start.6
  715.0 47.6 %collective-permute-start.6 = (bf16[2,32,18,1,128]{4,1,3,2,0:T(8,128)(2,1)}, bf16[2,32,18,1,128]{4,1,3,2,0:T(8,128)(2,1)}, u32[]{:S(2)}, u32[]{:S(2)}) collective-permute-start(bf16[2,32,18,1,128]{4,1,3,2,0:T(8,128)(2,1)} %get-tuple-element.431), channel_id=1, source_target_pairs={{0,1},{1,2},{2,3},{4,5},{5,6},{6,7},{8,9},{9,10},{10,11},{12,13},{... | collective-permute-start | bytes 884744 | tf_op jit(solution)/shard_map/ppermute | solution.py:15
  722.9 39.7 %collective-permute-start.7 = (bf16[2,32,18,1,128]{4,1,3,2,0:T(8,128)(2,1)S(1)}, bf16[2,32,18,1,128]{4,1,3,2,0:T(8,128)(2,1)}, u32[]{:S(2)}, u32[]{:S(2)}) collective-permute-start(bf16[2,32,18,1,128]{4,1,3,2,0:T(8,128)(2,1)S(1)} %get-tuple-element.432), channel_id=1, source_target_pairs={{1,0},{2,1},{3,2},{5,4},{6,5},{7,6},{9,8},{10,9},{11,10},{13,12},{... | collective-permute-start | bytes 884744 | tf_op jit(solution)/shard_map/ppermute | solution.py:16
  1782.1 25.6 %copy-start.20 = (bf16[32,16,16,128]{3,2,1,0:T(8,128)(2,1)S(1)}, bf16[32,16,16,128]{3,2,1,0:T(8,128)(2,1)}, u32[]{:S(2)}) copy-start(bf16[32,16,16,128]{3,2,1,0:T(8,128)(2,1)} %param.13) | copy-start | bytes 6291460
  1805.1 33.3 %collective-permute-start.8 = (bf16[1,32,1,16,128]{4,1,3,2,0:T(8,128)(2,1)S(1)}, bf16[1,32,1,16,128]{4,1,3,2,0:T(8,128)(2,1)S(1)}, u32[]{:S(2)}, u32[]{:S(2)}) collective-permute-start(bf16[1,32,1,16,128]{4,1,3,2,0:T(8,128)(2,1)S(1)} %get-tuple-element.429), channel_id=1, source_target_pairs={{0,4},{4,8},{8,12},{12,16},{16,20},{20,24},{24,28},{1,5},{5,9},{9,... | collective-permute-start | bytes 393224 | tf_op jit(solution)/shard_map/ppermute | solution.py:15
  1806.4 32.0 %collective-permute-start.9 = (bf16[1,32,1,16,128]{4,1,3,2,0:T(8,128)(2,1)S(1)}, bf16[1,32,1,16,128]{4,1,3,2,0:T(8,128)(2,1)S(1)}, u32[]{:S(2)}, u32[]{:S(2)}) collective-permute-start(bf16[1,32,1,16,128]{4,1,3,2,0:T(8,128)(2,1)S(1)} %get-tuple-element.430), channel_id=1, source_target_pairs={{4,0},{8,4},{12,8},{16,12},{20,16},{24,20},{28,24},{5,1},{9,5},{13... | collective-permute-start | bytes 393224 | tf_op jit(solution)/shard_map/ppermute | solution.py:16
  1814.1 24.3 %copy-start.18 = (bf16[1,32,16,16,128]{4,1,3,2,0:T(8,128)(2,1)}, bf16[1,32,16,16,128]{4,1,3,2,0:T(8,128)(2,1)S(1)}, u32[]{:S(2)}) copy-start(bf16[1,32,16,16,128]{4,1,3,2,0:T(8,128)(2,1)S(1)} %slice.1760) | copy-start | bytes 6291460
  1838.4 423.0 %all-reduce.22.cloned.1.call-start = ((), (), s32[]{:S(2)}) async-start(), calls=%async_computation | async-start | bytes 1769472 | tf_op jit(solution)/shard_map/psum | solution.py:228
  1838.5 56.9 %collective-permute-start.10 = (bf16[1,32,18,1,128]{4,1,3,2,0:T(8,128)(2,1)S(1)}, bf16[1,32,18,1,128]{4,1,3,2,0:T(8,128)(2,1)S(1)}, u32[]{:S(2)}, u32[]{:S(2)}) collective-permute-start(bf16[1,32,18,1,128]{4,1,3,2,0:T(8,128)(2,1)S(1)} %get-tuple-element.435), channel_id=1, source_target_pairs={{0,1},{1,2},{2,3},{4,5},{5,6},{6,7},{8,9},{9,10},{10,11},{12,13},{... | collective-permute-start | bytes 442376 | tf_op jit(solution)/shard_map/ppermute | solution.py:15
  1839.8 55.6 %collective-permute-start.11 = (bf16[1,32,18,1,128]{4,1,3,2,0:T(8,128)(2,1)S(1)}, bf16[1,32,18,1,128]{4,1,3,2,0:T(8,128)(2,1)S(1)}, u32[]{:S(2)}, u32[]{:S(2)}) collective-permute-start(bf16[1,32,18,1,128]{4,1,3,2,0:T(8,128)(2,1)S(1)} %get-tuple-element.436), channel_id=1, source_target_pairs={{1,0},{2,1},{3,2},{5,4},{6,5},{7,6},{9,8},{10,9},{11,10},{13,12},{... | collective-permute-start | bytes 442376 | tf_op jit(solution)/shard_map/ppermute | solution.py:16
  1895.4 8.2 copy-start.7
  1967.9 5.1 copy-start
  2007.5 5.1 copy-start
  2047.0 5.1 copy-start
  2086.6 5.1 copy-start
  2126.1 5.1 copy-start
  2165.7 5.1 copy-start
  2244.3 5.1 copy-start
  (96 other events, 219.5 us)
Sparse Core Ops, SparseCore 0:
  1838.5 56.8 all-reduce.23
  1898.7 55.1 all-reduce.21
